TPU v7x, 32 devices: a whole 2x2x4 slice. The times are simulated.
32 devices in a mesh: groups: 2 (over x), seq: 16 (over z, y, core).
Axes of the slice: x: 2, y: 2, z: 4, core: 2. Of those that a mesh axis runs over, the one named last changes fastest.
Arguments:
- tokens: bfloat16 [262144, 2048], P(('groups', 'seq')), parts along dimension 0, may hold values from -6 to 6
- right_blocks: bfloat16 [256, 512, 512], P('seq'), may hold values from -0.25 to 0.25
- left_blocks: bfloat16 [512, 256, 256], P('seq'), may hold values from -0.375 to 0.375
- chan_first: bfloat16 [32, 64, 64], replicated, may hold values from -0.75 to 0.75
- chan_second: bfloat16 [64, 32, 32], replicated, may hold values from -1 to 1
Outputs:
- mixed: bfloat16 [262144, 2048], P(('groups', 'seq')), parts along dimension 0
There are 2 independent parts, one for each index of `groups`. A program takes and returns all parts, laid end to end along the dimension named above; an argument that names none is the same for every part. Nothing has to cross between parts.
All inputs are finite; a program needn't handle non-finite values.
Results may differ from a plain program's by a relative error of at most 0.007.
Values may be sent and summed in bfloat16 or wider, within the bound.
A program may use at most 384 MiB of HBM per device.

v0:
```python
import jax
import jax.numpy as jnp
from jax import lax
from jax.sharding import PartitionSpec as P


def on_device(tokens, right_blocks, left_blocks, chan_first, chan_second):
    rows_a = right_blocks.shape[0]
    block_len = right_blocks.shape[1]
    width = tokens.shape[1]
    count_k = chan_first.shape[0]
    count_m = chan_first.shape[1]
    x = tokens.reshape(rows_a, block_len, width)
    first = jnp.einsum("aob,abc->aoc", right_blocks, x, preferred_element_type=jnp.float32).astype(
        jnp.bfloat16
    )
    turned = jnp.einsum(
        "bxa,abc->xbc",
        left_blocks,
        lax.all_to_all(first, "seq", split_axis=1, concat_axis=0, tiled=True),
        preferred_element_type=jnp.float32,
    ).astype(jnp.bfloat16)
    back = lax.all_to_all(turned, "seq", split_axis=0, concat_axis=1, tiled=True)
    hidden = back.reshape(rows_a * block_len, width)
    gated = (tokens.astype(jnp.float32) * hidden.astype(jnp.float32)).astype(jnp.bfloat16)
    grouped = gated.reshape(rows_a * block_len, count_k, count_m)
    chan_mid = jnp.einsum(
        "kom,skm->sko", chan_first, grouped, preferred_element_type=jnp.float32
    ).astype(jnp.bfloat16)
    result = jnp.einsum("mok,skm->som", chan_second, chan_mid, preferred_element_type=jnp.float32)
    return result.reshape(rows_a * block_len, width).astype(jnp.bfloat16)


def solution(mesh):
    return jax.shard_map(
        on_device,
        mesh=mesh,
        in_specs=(P(("groups", "seq"), None), P("seq", None, None), P("seq", None, None), P(), P()),
        out_specs=P(("groups", "seq"), None),
        check_vma=False,
    )
```

profile of v0, /device:TPU:15, one launch (start us, length us, event | category | flops | bytes accessed | tf_op | source)
XLA Modules:
  0.0 1969.9 jit_solution(11058670894132006757)
XLA Ops:
  0.0 0.0 copy-start
  0.0 32.4 %convolution_convert_fusion.1 = bf16[16,512,2048]{2,1,0:T(8,128)(2,1)} fusion(bf16[16,512,512]{2,1,0:T(8,128)(2,1)} %param.6, bf16[16,512,2048]{2,1,0:T(8,128)(2,1)} %bitcast.29), kind=kOutput, calls=%fused_computation.10 | convolution fusion | flops 17196646400 | bytes 75497472 | tf_op jit(solution)/shard_map/aob,abc->aoc/dot_general | solution.py:14
  32.4 30.0 %copy.34 = bf16[16,512,2048]{2,0,1:T(8,128)(2,1)} copy(bf16[16,512,2048]{2,1,0:T(8,128)(2,1)} %convolution_convert_fusion.1) | data formatting | bytes 67108864 | tf_op jit(solution)/shard_map/convert_element_type | solution.py:14
  62.5 729.7 %all_to_all.27 = bf16[16,512,2048]{2,0,1:T(8,128)(2,1)} all-to-all(bf16[16,512,2048]{2,0,1:T(8,128)(2,1)} %copy.34), channel_id=1, replica_groups=mesh['groups'=2,'seq'=16] {'seq'}, dimensions={1} | all-to-all | bytes 67108864 | tf_op jit(solution)/shard_map/all_to_all | solution.py:20
  792.2 29.9 %copy.36 = bf16[16,16,32,2048]{3,2,1,0:T(8,128)(2,1)} copy(bf16[16,16,32,2048]{3,1,2,0:T(8,128)(2,1)} %bitcast.27) | data formatting | bytes 67108864 | tf_op jit(solution)/shard_map/all_to_all | solution.py:20
  822.1 54.8 %convert_bitcast_fusion.2 = bf16[256,32,2048]{0,2,1:T(8,128)(2,1)} fusion(bf16[32,256,256]{2,1,0:T(8,128)(2,1)} %param.7, bf16[256,32,2048]{2,1,0:T(8,128)(2,1)} %bitcast.26), kind=kOutput, calls=%fused_computation.8 | convolution fusion | flops 8606711808 | bytes 71303168 | tf_op jit(solution)/shard_map/bxa,abc->xbc/dot_general | solution.py:17
  876.9 47.1 %copy.38 = bf16[256,32,2048]{2,1,0:T(8,128)(2,1)} copy(bf16[256,32,2048]{0,2,1:T(8,128)(2,1)} %convert_bitcast_fusion.2) | data formatting | bytes 67108864 | tf_op jit(solution)/shard_map/convert_element_type | solution.py:22
  924.1 0.0 copy-start.1
  924.1 5.9 all-to-all-start.1
  930.0 0.0 copy-done.1
  930.0 0.8 copy.42
  930.8 721.3 %all-to-all-done.1 = bf16[256,32,2048]{2,1,0:T(8,128)(2,1)} async-done(((bf16[256,32,2048]{2,1,0:T(8,128)(2,1)}), bf16[256,32,2048]{2,1,0:T(8,128)(2,1)}, u32[]{:S(2)}, u32[]{:S(2)}) %all-to-all-start.1) | async-done | bytes 33554464 | tf_op jit(solution)/shard_map/all_to_all | solution.py:23
  1652.1 32.4 %convert_bitcast_fusion = f32[16,16,32,2048]{3,2,0,1:T(8,128)} fusion(bf16[16,16,32,2048]{3,2,1,0:T(8,128)(2,1)} %bitcast.12), kind=kLoop, calls=%fused_computation | loop fusion | flops 16777216 | bytes 100663296 | tf_op jit(solution)/shard_map/convert_element_type | solution.py:25
  1684.6 43.8 %copy.39 = f32[16,16,32,2048]{3,2,1,0:T(8,128)} copy(f32[16,16,32,2048]{3,2,0,1:T(8,128)} %convert_bitcast_fusion) | data formatting | bytes 134217728 | tf_op jit(solution)/shard_map/convert_element_type | solution.py:25
  1728.4 42.5 %fusion = bf16[8192,2048]{1,0:T(8,128)(2,1)} fusion(f32[16,16,32,2048]{3,2,1,0:T(8,128)} %copy.39, bf16[8192,2048]{1,0:T(8,128)(2,1)} %param.5), kind=kLoop, calls=%fused_computation.2 | loop fusion | flops 50331648 | bytes 134217728 | tf_op jit(solution)/shard_map/convert_element_type | solution.py:25
  1770.9 40.6 %copy.40 = bf16[8192,2048]{0,1:T(8,128)(2,1)} copy(bf16[8192,2048]{1,0:T(8,128)(2,1)} %fusion) | data formatting | bytes 67108864 | tf_op jit(solution)/shard_map/convert_element_type | solution.py:25
  1811.5 0.0 copy-done
  1811.5 23.3 %convolution_convert_fusion = bf16[32,8192,64]{1,2,0:T(8,128)(2,1)} fusion(bf16[32,64,64]{2,1,0:T(8,128)(2,1)S(1)} %copy-done, bf16[8192,32,64]{0,2,1:T(8,128)(2,1)} %bitcast.25), kind=kOutput, calls=%fused_computation.9 | convolution fusion | flops 2164260864 | bytes 67371008 | tf_op jit(solution)/shard_map/kom,skm->sko/dot_general | solution.py:27
  1834.8 61.5 %convert_bitcast_fusion.1 = bf16[8192,32,64]{0,1,2:T(8,128)(2,1)} fusion(bf16[64,32,32]{2,1,0:T(8,128)(2,1)S(1)} %copy.42, bf16[32,8192,64]{1,2,0:T(8,128)(2,1)} %convolution_convert_fusion), kind=kOutput, calls=%fused_computation.7 | convolution fusion | flops 1090519040 | bytes 67239936 | tf_op jit(solution)/shard_map/mok,skm->som/dot_general | solution.py:30
  1896.3 29.4 %copy.43 = bf16[8192,32,64]{0,2,1:T(8,128)(2,1)} copy(bf16[8192,32,64]{0,1,2:T(8,128)(2,1)} %convert_bitcast_fusion.1) | data formatting | bytes 67108864 | tf_op jit(solution)/shard_map/convert_element_type | solution.py:31
  1925.7 44.2 %copy.44 = bf16[8192,2048]{1,0:T(8,128)(2,1)} copy(bf16[8192,2048]{0,1:T(8,128)(2,1)} %bitcast.28) | data formatting | bytes 67108864 | tf_op jit(solution)/shard_map/convert_element_type | solution.py:31
Async XLA Ops:
  0.0 1811.5 %copy-start = (bf16[32,64,64]{2,1,0:T(8,128)(2,1)S(1)}, bf16[32,64,64]{2,1,0:T(8,128)(2,1)}, u32[]{:S(2)}) copy-start(bf16[32,64,64]{2,1,0:T(8,128)(2,1)} %param.8) | copy-start | bytes 786436
  924.1 6.0 copy-start.1
  924.1 728.1 %all-to-all-start.1 = ((bf16[256,32,2048]{2,1,0:T(8,128)(2,1)}), bf16[256,32,2048]{2,1,0:T(8,128)(2,1)}, u32[]{:S(2)}, u32[]{:S(2)}) async-start(bf16[256,32,2048]{2,1,0:T(8,128)(2,1)} %copy.38), calls=%async_computation.1 | async-start | bytes 67108864 | tf_op jit(solution)/shard_map/all_to_all | solution.py:23
where the time goes:
time: 1970 us
  blocking collectives  730 us (37%)
  waiting for transfers between devices  721 us (37%)
  local copies, waits for them, and re-layouts  266 us (14%)
  matrix products  172 us (9%)
  other arithmetic  75 us (4%)
    all_to_all x1, blocking collectives, on_device(): lax.all_to_all(first, 'seq', split_axis=1, concat_axis=0, tiled=True)  730 us
    all_to_all x1, waiting for transfers between devices, on_device(): lax.all_to_all(turned, 'seq', split_axis=0, concat_axis=1, tiled=True)  721 us
    convert_element_type x2, local copies, waits for them, and re-layouts, on_device(): return result.reshape(rows_a * block_len, width).astype(jnp.bfloat16)  73.6 us
    dot_general x1, matrix products, on_device(): jnp.einsum('mok,skm->som', chan_second, chan_mid, preferred_element_type=...  61.5 us
    dot_general x1, matrix products, on_device(): jnp.einsum('bxa,abc->xbc', left_blocks, lax.all_to_all(first, 'seq', spli...  54.8 us
    convert_element_type x1, local copies, waits for them, and re-layouts, on_device(): turned = jnp.einsum('bxa,abc->xbc', left_blocks, lax.all_to_all(first, 's...  47.1 us
    convert_element_type x1, local copies, waits for them, and re-layouts, on_device(): hidden.astype(jnp.float32)  43.8 us
    convert_element_type x1, other arithmetic, on_device(): (tokens.astype(jnp.float32) * hidden.astype(jnp.float32)).astype(jnp.bflo...  42.5 us
  transfers between devices with their start and end apart: 1, of which 1 were waited for; matrix products, arithmetic and copies ran while one was open for 0% of the time, Pallas kernels for 0%

commit v1 on v0

v1 whole, which is shorter than its diff:
```python
import jax
import jax.numpy as jnp
from jax import lax
from jax.sharding import PartitionSpec as P

CHUNKS = 4


def on_device(devices, tokens, right_blocks, left_blocks, chan_first, chan_second):
    rows_a, block_len, _ = right_blocks.shape
    width = tokens.shape[1]
    count_k, count_m = chan_first.shape[0], chan_first.shape[1]
    own_b = left_blocks.shape[0]
    chunks = min(CHUNKS, own_b)
    part = own_b // chunks
    blocks = left_blocks.shape[1]
    mix = (
        chan_first.transpose(0, 2, 1)[:, :, None, :].astype(jnp.float32)
        * chan_second.transpose(2, 1, 0)[:, None, :, :].astype(jnp.float32)
    ).astype(jnp.bfloat16).reshape(width, width)
    x = tokens.reshape(rows_a, block_len, width)
    right = right_blocks.reshape(rows_a, devices, chunks, part, block_len)
    left = left_blocks.reshape(chunks, part, blocks, blocks)
    pieces = tokens.reshape(rows_a, devices, chunks, part, width)
    outs = []
    for j in range(chunks):
        first = jnp.einsum(
            "adib,abc->diac", right[:, :, j], x, preferred_element_type=jnp.float32
        ).astype(jnp.bfloat16)
        got = lax.all_to_all(first, "seq", split_axis=0, concat_axis=0, tiled=True)
        second = jnp.einsum(
            "ixsa,siac->xic",
            left[j].reshape(part, blocks, devices, rows_a),
            got,
            preferred_element_type=jnp.float32,
        ).astype(jnp.bfloat16)
        back = lax.all_to_all(
            second.reshape(devices, rows_a, part, width), "seq", split_axis=0, concat_axis=0, tiled=True
        )
        hidden = jnp.swapaxes(back, 0, 1)
        gated = (pieces[:, :, j].astype(jnp.float32) * hidden.astype(jnp.float32)).astype(jnp.bfloat16)
        outs.append(
            jnp.dot(gated.reshape(-1, width), mix, preferred_element_type=jnp.float32)
            .astype(jnp.bfloat16)
            .reshape(rows_a, devices, part, width)
        )
    return jnp.stack(outs, axis=2).reshape(rows_a * block_len, width)


def solution(mesh):
    devices = mesh.shape["seq"]

    def run(*args):
        return on_device(devices, *args)

    return jax.shard_map(
        run,
        mesh=mesh,
        in_specs=(P(("groups", "seq"), None), P("seq", None, None), P("seq", None, None), P(), P()),
        out_specs=P(("groups", "seq"), None),
        check_vma=False,
    )
```

time: 1970 us -> 1710 us (0.87)
  blocking collectives: 730 us -> 0 us
  waiting for transfers between devices: 721 us -> 1250 us
  local copies, waits for them, and re-layouts: 266 us -> 157 us
  starting transfers between devices: 5.94 us -> 44.3 us
    all_to_all x1 -> x0, blocking collectives: 730 us -> none  [on_device(): lax.all_to_all(first, 'seq', split_axis=1, concat_axis=0, tiled=True)]
    all_to_all x1 -> x8, waiting for transfers between devices: 721 us -> 1250 us  [the longest x4 629 us: on_device(): lax.all_to_all(second.reshape(devices, rows_a, part, width), 'seq', split...]
    convert_element_type x6 -> x7, local copies, waits for them, and re-layouts: 235 us -> 69.1 us  [the longest x4 45 us: on_device(): first = jnp.einsum('adib,abc->diac', right[:, :, j], x, preferred_element...]
    reshape x0 -> x4, local copies, waits for them, and re-layouts: none -> 51.7 us  [on_device(): second.reshape(devices, rows_a, part, width)]
    all_to_all x1 -> x8, starting transfers between devices: 5.94 us -> 44.3 us  [the longest x4 23 us: on_device(): got = lax.all_to_all(first, 'seq', split_axis=0, concat_axis=0, tiled=True)]
    convert_element_type x2 -> x4, other arithmetic: 75 us -> 41 us  [the longest x1 34.6 us: on_device(): (pieces[:, :, j].astype(jnp.float32) * hidden.astype(jnp.float32)).astype...]
    all_to_all x1 -> x0, local copies, waits for them, and re-layouts: 29.9 us -> none  [on_device(): lax.all_to_all(first, 'seq', split_axis=1, concat_axis=0, tiled=True)]
    another operation x0 -> x1, local copies, waits for them, and re-layouts: none -> 22.9 us  [on_device(): return jnp.stack(outs, axis=2).reshape(rows_a * block_len, width)]
  transfers between devices with their start and end apart: 1 -> 8, of which waited for: 1 -> 8; matrix products, arithmetic and copies ran while one was open for 0% -> 12% of each run, Pallas kernels for 0% -> 0%
where the time goes in v1:
time: 1710 us; the launch traced here: 1700 us
  waiting for transfers between devices  1250 us (73%)
  matrix products  186 us (11%)
  local copies, waits for them, and re-layouts  157 us (9%)
  other arithmetic  63.8 us (4%)
  starting transfers between devices  44.3 us (3%)
    all_to_all x4, waiting for transfers between devices, on_device(): lax.all_to_all(second.reshape(devices, rows_a, part, width), 'seq', split...  629 us
    all_to_all x4, waiting for transfers between devices, on_device(): got = lax.all_to_all(first, 'seq', split_axis=0, concat_axis=0, tiled=True)  619 us
    dot_general x4, matrix products, on_device(): jnp.dot(gated.reshape(-1, width), mix, preferred_element_type=jnp.float32)  82.4 us
    dot_general x4, matrix products, on_device(): jnp.einsum('adib,abc->diac', right[:, :, j], x, preferred_element_type=jn...  66.8 us
    reshape x4, local copies, waits for them, and re-layouts, on_device(): second.reshape(devices, rows_a, part, width)  51.7 us
    convert_element_type x4, local copies, waits for them, and re-layouts, on_device(): first = jnp.einsum('adib,abc->diac', right[:, :, j], x, preferred_element...  45 us
    dot_general x4, matrix products, on_device(): jnp.einsum('ixsa,siac->xic', left[j].reshape(part, blocks, devices, rows_...  36.6 us
    convert_element_type x1, other arithmetic, on_device(): (pieces[:, :, j].astype(jnp.float32) * hidden.astype(jnp.float32)).astype...  34.6 us
  transfers between devices with their start and end apart: 8, of which 8 were waited for; matrix products, arithmetic and copies ran while one was open for 12% of the time, Pallas kernels for 0%

profile of v1, /device:TPU:15, one launch (start us, length us, event | category | flops | bytes accessed | tf_op | source)
XLA Modules:
  0.0 1699.4 jit_solution(8406784094725521790)
XLA Ops:
  0.0 5.2 fusion.8
  5.2 17.9 %convert_bitcast_fusion.3 = bf16[16,8,16,2048]{3,0,2,1:T(8,128)(2,1)} fusion(bf16[16,512,2048,1]{2,1,0,3:T(8,128)(2,1)} %bitcast.108, bf16[16,16,1,8,512]{4,3,2,1,0:T(8,128)(2,1)S(1)} %get-tuple-element.9), kind=kOutput, calls=%fused_computation.21 | convolution fusion | flops 4299161600 | bytes 44040192 | tf_op jit(solution)/shard_map/adib,abc->diac/dot_general | solution.py:27
  23.1 11.2 copy.63
  34.3 7.0 all-to-all-start
  41.3 15.5 convert_bitcast_fusion.2
  56.8 11.3 copy.72
  68.1 155.4 %all-to-all-done = bf16[16,8,16,2048]{3,2,1,0:T(8,128)(2,1)} async-done(((bf16[16,8,16,2048]{3,2,1,0:T(8,128)(2,1)}), bf16[16,8,16,2048]{3,2,1,0:T(8,128)(2,1)}, u32[]{:S(2)}, u32[]{:S(2)}) %all-to-all-start) | async-done | bytes 8388640 | tf_op jit(solution)/shard_map/all_to_all | solution.py:30
  223.5 5.6 all-to-all-start.2
  229.1 15.5 convert_bitcast_fusion.1
  244.6 11.3 copy.79
  255.9 155.4 %all-to-all-done.2 = bf16[16,8,16,2048]{3,2,1,0:T(8,128)(2,1)} async-done(((bf16[16,8,16,2048]{3,2,1,0:T(8,128)(2,1)}), bf16[16,8,16,2048]{3,2,1,0:T(8,128)(2,1)}, u32[]{:S(2)}, u32[]{:S(2)}) %all-to-all-start.2) | async-done | bytes 8388640 | tf_op jit(solution)/shard_map/all_to_all | solution.py:30
  411.3 5.2 all-to-all-start.4
  416.5 17.9 %convert_bitcast_fusion = bf16[16,8,16,2048]{3,0,2,1:T(8,128)(2,1)} fusion(bf16[16,512,2048,1]{2,1,0,3:T(8,128)(2,1)} %bitcast.111, bf16[16,16,1,8,512]{4,3,2,1,0:T(8,128)(2,1)S(1)} %get-tuple-element.12), kind=kOutput, calls=%fused_computation.18 | convolution fusion | flops 4299161600 | bytes 44040192 | tf_op jit(solution)/shard_map/adib,abc->diac/dot_general | solution.py:27
  434.4 11.2 copy.86
  445.6 153.1 %all-to-all-done.4 = bf16[16,8,16,2048]{3,2,1,0:T(8,128)(2,1)} async-done(((bf16[16,8,16,2048]{3,2,1,0:T(8,128)(2,1)}), bf16[16,8,16,2048]{3,2,1,0:T(8,128)(2,1)}, u32[]{:S(2)}, u32[]{:S(2)}) %all-to-all-start.4) | async-done | bytes 8388640 | tf_op jit(solution)/shard_map/all_to_all | solution.py:30
  598.7 5.2 all-to-all-start.6
  604.0 3.9 fusion.9
  607.9 1.5 copy.106
  609.3 9.2 bitcast_convert_fusion.3
  618.5 12.9 copy.67
  631.4 154.8 %all-to-all-done.6 = bf16[16,8,16,2048]{3,2,1,0:T(8,128)(2,1)} async-done(((bf16[16,8,16,2048]{3,2,1,0:T(8,128)(2,1)}), bf16[16,8,16,2048]{3,2,1,0:T(8,128)(2,1)}, u32[]{:S(2)}, u32[]{:S(2)}) %all-to-all-start.6) | async-done | bytes 8388640 | tf_op jit(solution)/shard_map/all_to_all | solution.py:30
  786.2 5.3 all-to-all-start.1
  791.5 1.5 copy.108
  793.0 9.2 bitcast_convert_fusion.2
  802.1 12.9 copy.76
  815.0 158.7 %all-to-all-done.1 = bf16[16,16,8,2048]{3,2,1,0:T(8,128)(2,1)} async-done(((bf16[16,16,8,2048]{3,2,1,0:T(8,128)(2,1)}), bf16[16,16,8,2048]{3,2,1,0:T(8,128)(2,1)}, u32[]{:S(2)}, u32[]{:S(2)}) %all-to-all-start.1) | async-done | bytes 8388640 | tf_op jit(solution)/shard_map/all_to_all | solution.py:37
  973.7 5.5 all-to-all-start.3
  979.2 0.5 copy.110
  979.7 9.2 bitcast_convert_fusion.1
  988.9 12.9 copy.83
  1001.8 159.6 %all-to-all-done.3 = bf16[16,16,8,2048]{3,2,1,0:T(8,128)(2,1)} async-done(((bf16[16,16,8,2048]{3,2,1,0:T(8,128)(2,1)}), bf16[16,16,8,2048]{3,2,1,0:T(8,128)(2,1)}, u32[]{:S(2)}, u32[]{:S(2)}) %all-to-all-start.3) | async-done | bytes 8388640 | tf_op jit(solution)/shard_map/all_to_all | solution.py:37
  1161.4 5.2 all-to-all-start.5
  1166.6 0.5 copy.112
  1167.1 9.2 bitcast_convert_fusion
  1176.3 12.9 copy.90
  1189.2 0.0 copy-start.2
  1189.2 0.0 copy-start.3
  1189.2 159.6 %all-to-all-done.5 = bf16[16,16,8,2048]{3,2,1,0:T(8,128)(2,1)} async-done(((bf16[16,16,8,2048]{3,2,1,0:T(8,128)(2,1)}), bf16[16,16,8,2048]{3,2,1,0:T(8,128)(2,1)}, u32[]{:S(2)}, u32[]{:S(2)}) %all-to-all-start.5) | async-done | bytes 8388640 | tf_op jit(solution)/shard_map/all_to_all | solution.py:37
  1348.8 5.2 all-to-all-start.7
  1354.0 0.0 copy-done.2
  1354.1 0.1 convert_bitcast_fusion.4
  1354.2 0.3 copy.69
  1354.5 0.0 copy-done.3
  1354.5 0.1 convert_bitcast_fusion.5
  1354.6 0.3 copy.70
  1354.9 6.3 multiply_convert_fusion
  1361.2 23.5 %convert_element_type.173 = bf16[2048,2048]{1,0:T(8,128)(2,1)} reshape(bf16[32,64,32,64]{3,2,1,0:T(8,128)(2,1)} %multiply_convert_fusion) | data formatting | bytes 16777216 | tf_op jit(solution)/shard_map/convert_element_type | solution.py:20
  1384.6 151.6 %all-to-all-done.7 = bf16[16,16,8,2048]{3,2,1,0:T(8,128)(2,1)} async-done(((bf16[16,16,8,2048]{3,2,1,0:T(8,128)(2,1)}), bf16[16,16,8,2048]{3,2,1,0:T(8,128)(2,1)}, u32[]{:S(2)}, u32[]{:S(2)}) %all-to-all-start.7) | async-done | bytes 8388640 | tf_op jit(solution)/shard_map/all_to_all | solution.py:37
  1536.2 34.6 %fusion.3 = (bf16[16,16,8,2048]{3,2,1,0:T(8,128)(2,1)}, bf16[16,16,8,2048]{3,2,1,0:T(8,128)(2,1)}, bf16[16,16,8,2048]{3,2,1,0:T(8,128)(2,1)}, bf16[16,16,8,2048]{3,2,1,0:T(8,128)(2,1)}) fusion(bf16[16,16,4,8,2048]{4,3,2,1,0:T(8,128)(2,1)} %bitcast.112, bf16[16,16,8,2048]{3,2,1,0:T(8,128)(2,1)} %all-to-all-done.1, ...), kind=kLoop, calls=%fused_computation.9 | loop fusion | flops 67108864 | bytes 100663296 | tf_op jit(solution)/shard_map/convert_element_type | solution.py:41
  1570.9 0.0 copy-start.1
  1570.9 0.0 slice-start.2
  1570.9 23.7 %convolution_convert_fusion.3 = bf16[2048,2048]{1,0:T(8,128)(2,1)} fusion(bf16[2048,2048]{1,0:T(8,128)(2,1)} %bitcast.124, bf16[2048,2048]{1,0:T(8,128)(2,1)} %convert_element_type.173), kind=kOutput, calls=%fused_computation.25 | convolution fusion | flops 17184063488 | bytes 25165824 | tf_op jit(solution)/shard_map/dot_general | solution.py:43
  1594.6 0.0 copy-done
  1594.6 0.0 copy-done.1
  1594.6 0.0 slice-start
  1594.6 19.7 %convolution_convert_fusion.2 = bf16[2048,2048]{1,0:T(8,128)(2,1)} fusion(bf16[2048,2048]{1,0:T(8,128)(2,1)S(1)} %bitcast.123, bf16[2048,2048]{1,0:T(8,128)(2,1)S(1)} %copy-done), kind=kOutput, calls=%fused_computation.24 | convolution fusion | flops 17184063488 | bytes 25165824 | tf_op jit(solution)/shard_map/dot_general | solution.py:43
  1614.4 0.0 slice-done.2
  1614.4 0.0 slice-done.3
  1614.4 19.5 %convolution_convert_fusion.1 = bf16[2048,2048]{1,0:T(8,128)(2,1)} fusion(bf16[2048,2048]{1,0:T(8,128)(2,1)S(1)} %bitcast.122, bf16[2048,2048]{1,0:T(8,128)(2,1)S(1)} %copy-done), kind=kOutput, calls=%fused_computation.23 | convolution fusion | flops 17184063488 | bytes 25165824 | tf_op jit(solution)/shard_map/dot_general | solution.py:43
  1633.9 0.0 slice-done
  1633.9 0.0 slice-done.1
  1633.9 19.4 %convolution_convert_fusion = bf16[2048,2048]{1,0:T(8,128)(2,1)} fusion(bf16[2048,2048]{1,0:T(8,128)(2,1)S(1)} %bitcast.119, bf16[2048,2048]{1,0:T(8,128)(2,1)S(1)} %copy-done), kind=kOutput, calls=%fused_computation.22 | convolution fusion | flops 17184063488 | bytes 25165824 | tf_op jit(solution)/shard_map/dot_general | solution.py:43
  1653.3 22.7 %pad_maximum_fusion = bf16[16,16,4,8,2048]{4,3,1,0,2:T(8,128)(2,1)} fusion(bf16[16,16,1,8,2048]{4,3,1,0,2:T(8,128)(2,1)} %bitcast.129, bf16[16,16,1,8,2048]{4,3,1,0,2:T(8,128)(2,1)} %bitcast.128, bf16[16,16,1,8,2048]{4,3,1,0,2:T(8,128)(2,1)} %bitcast.127, bf16[16,16,1,8,2048]{4,3,1,0,2:T(8,128)(2,1)} %bitcast.126), kind=kLoop, calls=%fused_computation | loop fusion | flops 50331648 | bytes 67108864 | tf_op jit(solution)/shard_map/stack | solution.py:47
  1676.0 22.9 %copy.92 = bf16[16,16,4,8,2048]{4,3,2,1,0:T(8,128)(2,1)} copy(bf16[16,16,4,8,2048]{4,3,1,0,2:T(8,128)(2,1)} %pad_maximum_fusion) | data formatting | bytes 67108864 | tf_op jit(solution)/shard_map/stack | solution.py:47
  (5 shorter events, 0.0 us)
Async XLA Ops:
  34.3 189.2 %all-to-all-start = ((bf16[16,8,16,2048]{3,2,1,0:T(8,128)(2,1)}), bf16[16,8,16,2048]{3,2,1,0:T(8,128)(2,1)}, u32[]{:S(2)}, u32[]{:S(2)}) async-start(bf16[16,8,16,2048]{3,2,1,0:T(8,128)(2,1)} %copy.63), calls=%async_computation | async-start | bytes 16777216 | tf_op jit(solution)/shard_map/all_to_all | solution.py:30
  223.5 187.8 %all-to-all-start.2 = ((bf16[16,8,16,2048]{3,2,1,0:T(8,128)(2,1)}), bf16[16,8,16,2048]{3,2,1,0:T(8,128)(2,1)}, u32[]{:S(2)}, u32[]{:S(2)}) async-start(bf16[16,8,16,2048]{3,2,1,0:T(8,128)(2,1)} %copy.72), calls=%async_computation.2 | async-start | bytes 16777216 | tf_op jit(solution)/shard_map/all_to_all | solution.py:30
  411.3 187.4 %all-to-all-start.4 = ((bf16[16,8,16,2048]{3,2,1,0:T(8,128)(2,1)}), bf16[16,8,16,2048]{3,2,1,0:T(8,128)(2,1)}, u32[]{:S(2)}, u32[]{:S(2)}) async-start(bf16[16,8,16,2048]{3,2,1,0:T(8,128)(2,1)} %copy.79), calls=%async_computation.4 | async-start | bytes 16777216 | tf_op jit(solution)/shard_map/all_to_all | solution.py:30
  598.7 187.5 %all-to-all-start.6 = ((bf16[16,8,16,2048]{3,2,1,0:T(8,128)(2,1)}), bf16[16,8,16,2048]{3,2,1,0:T(8,128)(2,1)}, u32[]{:S(2)}, u32[]{:S(2)}) async-start(bf16[16,8,16,2048]{3,2,1,0:T(8,128)(2,1)} %copy.86), calls=%async_computation.6 | async-start | bytes 16777216 | tf_op jit(solution)/shard_map/all_to_all | solution.py:30
  786.2 187.5 %all-to-all-start.1 = ((bf16[16,16,8,2048]{3,2,1,0:T(8,128)(2,1)}), bf16[16,16,8,2048]{3,2,1,0:T(8,128)(2,1)}, u32[]{:S(2)}, u32[]{:S(2)}) async-start(bf16[16,16,8,2048]{3,2,1,0:T(8,128)(2,1)} %copy.67), calls=%async_computation.1 | async-start | bytes 16777216 | tf_op jit(solution)/shard_map/all_to_all | solution.py:37
  973.7 187.7 %all-to-all-start.3 = ((bf16[16,16,8,2048]{3,2,1,0:T(8,128)(2,1)}), bf16[16,16,8,2048]{3,2,1,0:T(8,128)(2,1)}, u32[]{:S(2)}, u32[]{:S(2)}) async-start(bf16[16,16,8,2048]{3,2,1,0:T(8,128)(2,1)} %copy.76), calls=%async_computation.3 | async-start | bytes 16777216 | tf_op jit(solution)/shard_map/all_to_all | solution.py:37
  1161.4 187.4 %all-to-all-start.5 = ((bf16[16,16,8,2048]{3,2,1,0:T(8,128)(2,1)}), bf16[16,16,8,2048]{3,2,1,0:T(8,128)(2,1)}, u32[]{:S(2)}, u32[]{:S(2)}) async-start(bf16[16,16,8,2048]{3,2,1,0:T(8,128)(2,1)} %copy.83), calls=%async_computation.5 | async-start | bytes 16777216 | tf_op jit(solution)/shard_map/all_to_all | solution.py:37
  1189.2 164.8 %copy-start.2 = (bf16[32,64,64]{2,1,0:T(8,128)(2,1)S(1)}, bf16[32,64,64]{2,1,0:T(8,128)(2,1)}, u32[]{:S(2)}) copy-start(bf16[32,64,64]{2,1,0:T(8,128)(2,1)} %param.8) | copy-start | bytes 786436
  1189.2 165.3 %copy-start.3 = (bf16[64,32,32]{0,2,1:T(8,128)(2,1)S(1)}, bf16[64,32,32]{0,2,1:T(8,128)(2,1)}, u32[]{:S(2)}) copy-start(bf16[64,32,32]{0,2,1:T(8,128)(2,1)} %param.9) | copy-start | bytes 393220
  1348.8 187.5 %all-to-all-start.7 = ((bf16[16,16,8,2048]{3,2,1,0:T(8,128)(2,1)}), bf16[16,16,8,2048]{3,2,1,0:T(8,128)(2,1)}, u32[]{:S(2)}, u32[]{:S(2)}) async-start(bf16[16,16,8,2048]{3,2,1,0:T(8,128)(2,1)} %copy.90), calls=%async_computation.7 | async-start | bytes 16777216 | tf_op jit(solution)/shard_map/all_to_all | solution.py:37
  1570.9 23.8 %copy-start = (bf16[2048,2048]{1,0:T(8,128)(2,1)S(1)}, bf16[2048,2048]{1,0:T(8,128)(2,1)}, u32[]{:S(2)}) copy-start(bf16[2048,2048]{1,0:T(8,128)(2,1)} %convert_element_type.173) | copy-start | bytes 25165828
  1570.9 23.8 %copy-start.1 = (bf16[16,16,8,2048]{3,2,1,0:T(8,128)(2,1)S(1)}, bf16[16,16,8,2048]{3,2,1,0:T(8,128)(2,1)}, u32[]{:S(2)}) copy-start(bf16[16,16,8,2048]{3,2,1,0:T(8,128)(2,1)} %get-tuple-element.8) | copy-start | bytes 25165828
  1570.9 43.5 %slice-start.2 = ((s8[8388608]{0:T(1024)(128)(4,1)}), s8[4194304]{0:T(1024)(128)(4,1)S(1)}, s32[]{:S(2)}) async-start(s8[8388608]{0:T(1024)(128)(4,1)} %bitcast.120), calls=%async_computation.10 | async-start | bytes 8388608
  1594.6 19.8 %slice-start.3 = ((s8[8388608]{0:T(1024)(128)(4,1)}), s8[4194304]{0:T(1024)(128)(4,1)S(1)}, s32[]{:S(2)}) async-start(s8[8388608]{0:T(1024)(128)(4,1)} %bitcast.120), calls=%async_computation.11 | async-start | bytes 8388608
  1594.6 39.3 %slice-start = ((s8[8388608]{0:T(1024)(128)(4,1)}), s8[4194304]{0:T(1024)(128)(4,1)S(1)}, s32[]{:S(2)}) async-start(s8[8388608]{0:T(1024)(128)(4,1)} %bitcast.117), calls=%async_computation.8 | async-start | bytes 8388608
  1614.4 19.5 %slice-start.1 = ((s8[8388608]{0:T(1024)(128)(4,1)}), s8[4194304]{0:T(1024)(128)(4,1)S(1)}, s32[]{:S(2)}) async-start(s8[8388608]{0:T(1024)(128)(4,1)} %bitcast.117), calls=%async_computation.9 | async-start | bytes 8388608

commit v2 on v1

v2 whole, which is shorter than its diff:
```python
import jax
import jax.numpy as jnp
from jax import lax
from jax.experimental import pallas as pl
from jax.experimental.pallas import tpu as pltpu
from jax.sharding import PartitionSpec as P


def chunk_list(own_b):
    if own_b % 32 == 0:
        quarter = own_b // 4
        return [(0, quarter), (2 * quarter, 2 * quarter), (quarter, quarter)]
    return [(0, own_b)]


def gate_mix(tokens, hidden, mix, out, start, rows_step):
    rows_a, devices, _, width = tokens.shape
    part = hidden.shape[2]
    rows = rows_step * devices * part

    def kernel(tokens_ref, hidden_ref, mix_ref, *refs):
        out_ref = refs[-1]
        for r in range(rows_step):
            gated = tokens_ref[r].astype(jnp.float32) * hidden_ref[:, r].astype(jnp.float32)
            gated = gated.reshape(rows // rows_step, width).astype(jnp.bfloat16)
            res = jnp.dot(gated, mix_ref[...], preferred_element_type=jnp.float32)
            out_ref[r] = res.reshape(devices, part, width).astype(jnp.bfloat16)

    own = pl.BlockSpec((rows_step, devices, part, width), lambda a: (a, 0, start // part, 0))
    in_specs = [
        own,
        pl.BlockSpec((devices, rows_step, part, width), lambda a: (0, a, 0, 0)),
        pl.BlockSpec((width, width), lambda a: (0, 0)),
    ]
    operands = [tokens, hidden, mix]
    aliases = {}
    if out is not None:
        in_specs.append(pl.BlockSpec(memory_space=pl.ANY))
        operands.append(out)
        aliases = {3: 0}
    total = rows_a * devices * part
    return pl.pallas_call(
        kernel,
        grid=(rows_a // rows_step,),
        in_specs=in_specs,
        out_specs=own,
        out_shape=jax.ShapeDtypeStruct(tokens.shape, jnp.bfloat16),
        input_output_aliases=aliases,
        compiler_params=pltpu.CompilerParams(vmem_limit_bytes=56 * 2**20),
        cost_estimate=pl.CostEstimate(
            flops=2 * total * width * width,
            bytes_accessed=6 * total * width + 2 * width * width,
            transcendentals=0,
        ),
        name="gate_mix",
    )(*operands)


def on_device(devices, tokens, right_blocks, left_blocks, chan_first, chan_second):
    rows_a, block_len, _ = right_blocks.shape
    width = tokens.shape[1]
    own_b = left_blocks.shape[0]
    blocks = left_blocks.shape[1]
    mix = (
        chan_first.transpose(0, 2, 1)[:, :, None, :].astype(jnp.float32)
        * chan_second.transpose(2, 1, 0)[:, None, :, :].astype(jnp.float32)
    ).astype(jnp.bfloat16).reshape(width, width)
    x = tokens.reshape(rows_a, block_len, width)
    right = right_blocks.reshape(rows_a, devices, own_b, block_len)
    pieces = tokens.reshape(rows_a, devices, own_b, width)
    out = None
    for start, part in chunk_list(own_b):
        first = jnp.einsum(
            "adib,abc->diac", right[:, :, start : start + part], x, preferred_element_type=jnp.float32
        ).astype(jnp.bfloat16)
        got = lax.all_to_all(first, "seq", split_axis=0, concat_axis=0, tiled=True)
        second = jnp.einsum(
            "ixsa,siac->xic",
            left_blocks[start : start + part].reshape(part, blocks, devices, rows_a),
            got,
            preferred_element_type=jnp.float32,
        ).astype(jnp.bfloat16)
        back = lax.all_to_all(
            second.reshape(devices, rows_a, part, width), "seq", split_axis=0, concat_axis=0, tiled=True
        )
        if part % 8 == 0:
            rows_step = 2 if part == 8 and rows_a % 2 == 0 else 1
            out = gate_mix(pieces, back, mix, out, start, rows_step)
        else:
            hidden = jnp.swapaxes(back, 0, 1)
            gated = (pieces.astype(jnp.float32) * hidden.astype(jnp.float32)).astype(jnp.bfloat16)
            out = jnp.dot(gated.reshape(-1, width), mix, preferred_element_type=jnp.float32).astype(
                jnp.bfloat16
            )
    return out.reshape(rows_a * block_len, width)


def solution(mesh):
    devices = mesh.shape["seq"]

    def run(*args):
        return on_device(devices, *args)

    return jax.shard_map(
        run,
        mesh=mesh,
        in_specs=(P(("groups", "seq"), None), P("seq", None, None), P("seq", None, None), P(), P()),
        out_specs=P(("groups", "seq"), None),
        check_vma=False,
    )
```

time: 1710 us -> 1550 us (0.906)
  matrix products: 186 us -> 89.2 us
  Pallas kernels: 0 us -> 90.9 us
  other arithmetic: 63.8 us -> 6.44 us
  waiting for transfers between devices: 1250 us -> 1200 us
  local copies, waits for them, and re-layouts: 157 us -> 122 us
    dot_general x12 -> x6, matrix products: 186 us -> 89.2 us  [the longest x3 57.5 us: on_device(): jnp.einsum('adib,abc->diac', right[:, :, start:start + part], x, preferre...]
    pallas_call x0 -> x3, Pallas kernels: none -> 90.9 us  [gate_mix(): pl.pallas_call(kernel, grid=(rows_a // rows_step,), in_specs=in_specs, ou...]
    all_to_all x4 -> x3, waiting for transfers between devices: 629 us -> 570 us  [on_device(): lax.all_to_all(second.reshape(devices, rows_a, part, width), 'seq', split...]
    reshape x4 -> x0, local copies, waits for them, and re-layouts: 51.7 us -> none  [on_device(): second.reshape(devices, rows_a, part, width)]
    convert_element_type x4 -> x6, local copies, waits for them, and re-layouts: 45 us -> 82.1 us  [the longest x3 41 us: on_device(): first = jnp.einsum('adib,abc->diac', right[:, :, start:start + part], x,...]
    convert_element_type x1 -> x0, other arithmetic: 34.6 us -> none  [on_device(): (pieces[:, :, j].astype(jnp.float32) * hidden.astype(jnp.float32)).astype...]
    another operation x1 -> x0, local copies, waits for them, and re-layouts: 22.9 us -> none  [on_device(): return jnp.stack(outs, axis=2).reshape(rows_a * block_len, width)]
    another operation x1 -> x0, other arithmetic: 22.7 us -> none  [on_device(): return jnp.stack(outs, axis=2).reshape(rows_a * block_len, width)]
  transfers between devices with their start and end apart: 8 -> 6, of which waited for: 8 -> 6; matrix products, arithmetic and copies ran while one was open for 12% -> 12% of each run, Pallas kernels for 0% -> 4%
where the time goes in v2:
time: 1550 us; the launch traced here: 1540 us
  waiting for transfers between devices  1200 us (77%)
  local copies, waits for them, and re-layouts  122 us (8%)
  Pallas kernels  90.9 us (6%)
  matrix products  89.2 us (6%)
  starting transfers between devices  32.9 us (2%)
    all_to_all x3, waiting for transfers between devices, on_device(): got = lax.all_to_all(first, 'seq', split_axis=0, concat_axis=0, tiled=True)  630 us
    all_to_all x3, waiting for transfers between devices, on_device(): lax.all_to_all(second.reshape(devices, rows_a, part, width), 'seq', split...  570 us
    pallas_call x3, Pallas kernels, gate_mix(): pl.pallas_call(kernel, grid=(rows_a // rows_step,), in_specs=in_specs, ou...  90.9 us
    dot_general x3, matrix products, on_device(): jnp.einsum('adib,abc->diac', right[:, :, start:start + part], x, preferre...  57.5 us
    convert_element_type x3, local copies, waits for them, and re-layouts, on_device(): first = jnp.einsum('adib,abc->diac', right[:, :, start:start + part], x,...  41 us
    convert_element_type x3, local copies, waits for them, and re-layouts, on_device(): second = jnp.einsum('ixsa,siac->xic', left_blocks[start:start + part].res...  41 us
    dot_general x3, matrix products, on_device(): jnp.einsum('ixsa,siac->xic', left_blocks[start:start + part].reshape(part...  31.6 us
  transfers between devices with their start and end apart: 6, of which 6 were waited for; matrix products, arithmetic and copies ran while one was open for 12% of the time, Pallas kernels for 4%

profile of v2, /device:TPU:15, one launch (start us, length us, event | category | flops | bytes accessed | tf_op | source)
XLA Modules:
  0.0 1542.0 jit_solution(11257567555563794720)
XLA Ops:
  0.0 2.6 fusion.9
  2.6 17.9 %convert_bitcast_fusion.1 = bf16[16,8,16,2048]{3,0,2,1:T(8,128)(2,1)} fusion(bf16[16,512,2048,1]{2,1,0,3:T(8,128)(2,1)} %bitcast.48, bf16[16,16,8,512]{3,2,1,0:T(8,128)(2,1)S(1)} %get-tuple-element.5), kind=kOutput, calls=%fused_computation.8 | convolution fusion | flops 4299161600 | bytes 44040192 | tf_op jit(solution)/shard_map/adib,abc->diac/dot_general | solution.py:73
  20.5 11.3 copy.54
  31.8 7.2 all-to-all-start.4
  39.0 4.8 slice.25
  43.7 17.9 %convert_bitcast_fusion.2 = bf16[16,8,16,2048]{3,0,2,1:T(8,128)(2,1)} fusion(bf16[16,512,2048,1]{2,1,0,3:T(8,128)(2,1)} %bitcast.49, bf16[16,16,8,512]{3,2,1,0:T(8,128)(2,1)S(1)} %get-tuple-element.6), kind=kOutput, calls=%fused_computation.9 | convolution fusion | flops 4299161600 | bytes 44040192 | tf_op jit(solution)/shard_map/adib,abc->diac/dot_general | solution.py:73
  61.6 11.2 copy.42
  72.8 148.3 %all-to-all-done.4 = bf16[16,8,16,2048]{3,2,1,0:T(8,128)(2,1)} async-done(((bf16[16,8,16,2048]{3,2,1,0:T(8,128)(2,1)}), bf16[16,8,16,2048]{3,2,1,0:T(8,128)(2,1)}, u32[]{:S(2)}, u32[]{:S(2)}) %all-to-all-start.4) | async-done | bytes 8388640 | tf_op jit(solution)/shard_map/all_to_all | solution.py:76
  221.1 4.9 all-to-all-start
  226.0 21.8 %convert_bitcast_fusion = bf16[16,16,16,2048]{3,0,2,1:T(8,128)(2,1)} fusion(bf16[16,512,2048,1]{2,1,0,3:T(8,128)(2,1)} %bitcast.50, bf16[16,16,16,512]{3,2,1,0:T(8,128)(2,1)} %slice.25), kind=kOutput, calls=%fused_computation.4 | convolution fusion | flops 8598323200 | bytes 54525952 | tf_op jit(solution)/shard_map/adib,abc->diac/dot_general | solution.py:73
  247.8 18.6 %copy.49 = bf16[16,16,16,2048]{3,2,1,0:T(8,128)(2,1)} copy(bf16[16,16,16,2048]{3,0,2,1:T(8,128)(2,1)} %convert_bitcast_fusion) | data formatting | bytes 33554432 | tf_op jit(solution)/shard_map/convert_element_type | solution.py:75
  266.4 142.0 %all-to-all-done = bf16[16,8,16,2048]{3,2,1,0:T(8,128)(2,1)} async-done(((bf16[16,8,16,2048]{3,2,1,0:T(8,128)(2,1)}), bf16[16,8,16,2048]{3,2,1,0:T(8,128)(2,1)}, u32[]{:S(2)}, u32[]{:S(2)}) %all-to-all-start) | async-done | bytes 8388640 | tf_op jit(solution)/shard_map/all_to_all | solution.py:76
  408.4 5.3 all-to-all-start.2
  413.6 1.7 fusion.10
  415.3 0.5 copy.63
  415.9 9.2 fusion.2
  425.0 11.2 copy.57
  436.3 339.3 %all-to-all-done.2 = bf16[16,16,16,2048]{3,2,1,0:T(8,128)(2,1)} async-done(((bf16[16,16,16,2048]{3,2,1,0:T(8,128)(2,1)}), bf16[16,16,16,2048]{3,2,1,0:T(8,128)(2,1)}, u32[]{:S(2)}, u32[]{:S(2)}) %all-to-all-start.2) | async-done | bytes 16777248 | tf_op jit(solution)/shard_map/all_to_all | solution.py:76
  775.6 4.9 all-to-all-start.5
  780.5 3.1 slice.21
  783.6 2.8 copy.61
  786.4 13.3 fusion
  799.7 18.6 %copy.52 = bf16[256,16,2048]{2,1,0:T(8,128)(2,1)} copy(bf16[256,16,2048]{2,0,1:T(8,128)(2,1)} %fusion) | data formatting | bytes 33554432 | tf_op jit(solution)/shard_map/convert_element_type | solution.py:82
  818.3 144.5 %all-to-all-done.5.hidden_ref = bf16[16,16,8,2048]{3,2,1,0:T(8,128)(2,1)} async-done(((bf16[16,16,8,2048]{3,2,1,0:T(8,128)(2,1)}), bf16[16,16,8,2048]{3,2,1,0:T(8,128)(2,1)}, u32[]{:S(2)}, u32[]{:S(2)}) %all-to-all-start.5) | async-done | bytes 8388640 | tf_op jit(solution)/shard_map/all_to_all | solution.py:83
  962.8 5.3 all-to-all-start.3
  968.1 0.5 copy.59
  968.7 9.2 fusion.1
  977.8 11.2 copy.45
  989.0 341.0 %all-to-all-done.3.hidden_ref = bf16[16,16,16,2048]{3,2,1,0:T(8,128)(2,1)} async-done(((bf16[16,16,16,2048]{3,2,1,0:T(8,128)(2,1)}), bf16[16,16,16,2048]{3,2,1,0:T(8,128)(2,1)}, u32[]{:S(2)}, u32[]{:S(2)}) %all-to-all-start.3) | async-done | bytes 16777248 | tf_op jit(solution)/shard_map/all_to_all | solution.py:83
  1330.1 0.0 copy-start
  1330.1 0.0 copy-start.1
  1330.1 5.4 all-to-all-start.1
  1335.5 0.0 copy-done
  1335.5 0.1 convert_bitcast_fusion.3
  1335.6 0.3 copy.46
  1336.0 0.0 copy-done.1
  1336.0 0.1 convert_bitcast_fusion.4
  1336.0 0.3 copy.47
  1336.3 6.3 multiply_convert_fusion
  1342.6 23.4 %convert_element_type.66.mix_ref = bf16[2048,2048]{1,0:T(8,128)(2,1)} reshape(bf16[32,64,32,64]{3,2,1,0:T(8,128)(2,1)} %multiply_convert_fusion) | data formatting | bytes 16777216 | tf_op jit(solution)/shard_map/convert_element_type | solution.py:67
  1366.1 24.0 %gate_mix.3.refs_0_ = bf16[16,16,32,2048]{3,2,1,0:T(8,128)(2,1)} custom-call(bf16[16,16,32,2048]{3,2,1,0:T(8,128)(2,1)} %bitcast.51, bf16[16,16,8,2048]{3,2,1,0:T(8,128)(2,1)} %all-to-all-done.5.hidden_ref, bf16[2048,2048]{1,0:T(8,128)(2,1)} %convert_element_type.66.mix_ref), custom_call_target="tpu_custom_call" | custom-call | flops 17179869184 | bytes 33554432 | tf_op jit(solution)/shard_map/gate_mix/pallas_call | solution.py:42
  1390.1 42.9 %gate_mix.4.refs_0_ = bf16[16,16,32,2048]{3,2,1,0:T(8,128)(2,1)} custom-call(bf16[16,16,32,2048]{3,2,1,0:T(8,128)(2,1)} %bitcast.52, bf16[16,16,16,2048]{3,2,1,0:T(8,128)(2,1)} %all-to-all-done.3.hidden_ref, bf16[2048,2048]{1,0:T(8,128)(2,1)} %convert_element_type.66.mix_ref, bf16[16,16,32,2048]{3,2,1,0:T(8,128)(2,1)} %gate_mix.3.refs_0_), custom_call_target="tpu_custom_call", output_to_operand_aliasing={{}: (3, {})} | custom-call | flops 34359738368 | bytes 58720256 | tf_op jit(solution)/shard_map/gate_mix/pallas_call | solution.py:42
  1433.0 84.7 %all-to-all-done.1.hidden_ref = bf16[16,16,8,2048]{3,2,1,0:T(8,128)(2,1)} async-done(((bf16[16,16,8,2048]{3,2,1,0:T(8,128)(2,1)}), bf16[16,16,8,2048]{3,2,1,0:T(8,128)(2,1)}, u32[]{:S(2)}, u32[]{:S(2)}) %all-to-all-start.1) | async-done | bytes 8388640 | tf_op jit(solution)/shard_map/all_to_all | solution.py:83
  1517.7 24.0 %gate_mix.5 = bf16[16,16,32,2048]{3,2,1,0:T(8,128)(2,1)} custom-call(bf16[16,16,32,2048]{3,2,1,0:T(8,128)(2,1)} %bitcast.53, bf16[16,16,8,2048]{3,2,1,0:T(8,128)(2,1)} %all-to-all-done.1.hidden_ref, bf16[2048,2048]{1,0:T(8,128)(2,1)} %convert_element_type.66.mix_ref, bf16[16,16,32,2048]{3,2,1,0:T(8,128)(2,1)} %gate_mix.4.refs_0_), custom_call_target="tpu_custom_call", output_to_operand_aliasing={{}: (3, {})} | custom-call | flops 17179869184 | bytes 33554432 | tf_op jit(solution)/shard_map/gate_mix/pallas_call | solution.py:42
Async XLA Ops:
  31.8 189.4 %all-to-all-start.4 = ((bf16[16,8,16,2048]{3,2,1,0:T(8,128)(2,1)}), bf16[16,8,16,2048]{3,2,1,0:T(8,128)(2,1)}, u32[]{:S(2)}, u32[]{:S(2)}) async-start(bf16[16,8,16,2048]{3,2,1,0:T(8,128)(2,1)} %copy.54), calls=%async_computation.4 | async-start | bytes 16777216 | tf_op jit(solution)/shard_map/all_to_all | solution.py:76
  221.1 187.2 %all-to-all-start = ((bf16[16,8,16,2048]{3,2,1,0:T(8,128)(2,1)}), bf16[16,8,16,2048]{3,2,1,0:T(8,128)(2,1)}, u32[]{:S(2)}, u32[]{:S(2)}) async-start(bf16[16,8,16,2048]{3,2,1,0:T(8,128)(2,1)} %copy.42), calls=%async_computation | async-start | bytes 16777216 | tf_op jit(solution)/shard_map/all_to_all | solution.py:76
  408.4 367.2 %all-to-all-start.2 = ((bf16[16,16,16,2048]{3,2,1,0:T(8,128)(2,1)}), bf16[16,16,16,2048]{3,2,1,0:T(8,128)(2,1)}, u32[]{:S(2)}, u32[]{:S(2)}) async-start(bf16[16,16,16,2048]{3,2,1,0:T(8,128)(2,1)} %copy.49), calls=%async_computation.2 | async-start | bytes 33554432 | tf_op jit(solution)/shard_map/all_to_all | solution.py:76
  775.6 187.2 %all-to-all-start.5 = ((bf16[16,16,8,2048]{3,2,1,0:T(8,128)(2,1)}), bf16[16,16,8,2048]{3,2,1,0:T(8,128)(2,1)}, u32[]{:S(2)}, u32[]{:S(2)}) async-start(bf16[16,16,8,2048]{3,2,1,0:T(8,128)(2,1)} %bitcast.56), calls=%async_computation.5 | async-start | bytes 16777216 | tf_op jit(solution)/shard_map/all_to_all | solution.py:83
  962.8 367.2 %all-to-all-start.3 = ((bf16[16,16,16,2048]{3,2,1,0:T(8,128)(2,1)}), bf16[16,16,16,2048]{3,2,1,0:T(8,128)(2,1)}, u32[]{:S(2)}, u32[]{:S(2)}) async-start(bf16[16,16,16,2048]{3,2,1,0:T(8,128)(2,1)} %bitcast.54), calls=%async_computation.3 | async-start | bytes 33554432 | tf_op jit(solution)/shard_map/all_to_all | solution.py:83
  1330.1 5.4 copy-start
  1330.1 5.9 copy-start.1
  1330.1 187.6 %all-to-all-start.1 = ((bf16[16,16,8,2048]{3,2,1,0:T(8,128)(2,1)}), bf16[16,16,8,2048]{3,2,1,0:T(8,128)(2,1)}, u32[]{:S(2)}, u32[]{:S(2)}) async-start(bf16[16,16,8,2048]{3,2,1,0:T(8,128)(2,1)} %bitcast.55), calls=%async_computation.1 | async-start | bytes 16777216 | tf_op jit(solution)/shard_map/all_to_all | solution.py:83
